TPU v7x, 32 devices: a whole 2x2x4 slice. The times are simulated.
32 devices in a mesh: seq: 8 (over z, y), head: 4 (over x, core).
Axes of the slice: x: 2, y: 2, z: 4, core: 2. Of those that a mesh axis runs over, the one named last changes fastest.
Arguments:
- queries: bfloat16 [8192, 2048], P('seq', 'head'), may hold values from -100 to 100
- values: bfloat16 [8192, 2048], P('seq', 'head'), may hold values from -6 to 6
- codes: int32 [8192, 16], P('seq', 'head'), may hold values from 0 to 511
- codebook: bfloat16 [16, 512, 128], P('head'), may hold values from -4 to 4
- out_weight: bfloat16 [2048, 2048], P('head'), may hold values from -0.125 to 0.125
- grad_out: bfloat16 [8192, 2048], P('seq', 'head'), may hold values from -6 to 6
Outputs:
- grad_queries: bfloat16 [8192, 2048], P('seq', 'head')
- grad_values: bfloat16 [8192, 2048], P('seq', 'head')
- grad_codebook: float32 [16, 512, 128], P('head')
All inputs are finite; a program needn't handle non-finite values.
Results may differ from a plain program's by a relative error of at most 0.012.
The roundings to bfloat16 on the way count: a program that leaves them out, or rounds other values in their place, can miss the bound.
Values may be sent and summed in bfloat16 or wider, within the bound.
A program may use at most 192 MiB of HBM per device.

v0:
```python
from functools import reduce

import jax
import jax.numpy as jnp
from jax import lax
from jax.sharding import PartitionSpec as P

BLOCK = 512


def entering(array, axis, combine, identity, reverse):
    count, here = (lax.axis_size(axis), lax.axis_index(axis))
    everything = jax.tree.map(lambda part: lax.all_gather(part, axis), array)
    start = jax.tree.map(
        lambda part, zero: jnp.broadcast_to(jnp.asarray(zero, part.dtype), part.shape),
        array,
        identity,
    )

    def hop(k, before):
        at = count - 1 - k if reverse else k
        reached = at > here if reverse else at < here
        new = combine(before, jax.tree.map(lambda part: part[at], everything))
        return jax.tree.map(lambda a, b: jnp.where(reached, a, b), new, before)

    return lax.fori_loop(0, count, hop, start)


def add_tree(earlier, later):
    return jax.tree.map(jnp.add, earlier, later)


def attend_block(query, value, onehot, dout, codebook, prefix_values, prefix_counts):
    block_rows, heads_here, head_width = query.shape
    scale = head_width ** (-0.5)
    keys = jnp.einsum("ths,hse->the", onehot, codebook, preferred_element_type=jnp.float32).astype(
        jnp.bfloat16
    )
    scores = jnp.einsum("the,uhe->htu", query, keys, preferred_element_type=jnp.float32) * scale
    positions = lax.iota(jnp.int32, block_rows)
    causal = positions[:, None] >= positions[None, :]
    cache_scores = (
        jnp.einsum("the,hce->htc", query, codebook, preferred_element_type=jnp.float32) * scale
    )
    counts_row = prefix_counts[:, None, :]
    present = counts_row > 0.0
    highest = jnp.maximum(
        jnp.max(jnp.where(causal, scores, -jnp.inf), axis=-1, keepdims=True),
        jnp.max(jnp.where(present, cache_scores, -jnp.inf), axis=-1, keepdims=True),
    )
    local_exp = jnp.where(causal, jnp.exp(jnp.where(causal, scores - highest, 0.0)), 0.0)
    cache_exp = jnp.where(present, jnp.exp(jnp.where(present, cache_scores - highest, 0.0)), 0.0)
    total = jnp.sum(local_exp, axis=-1, keepdims=True) + jnp.sum(
        cache_exp * counts_row, axis=-1, keepdims=True
    )
    local_prob = local_exp / total
    cache_prob = cache_exp / total
    local_low = local_prob.astype(jnp.bfloat16)
    cache_low = cache_prob.astype(jnp.bfloat16)
    cache_values = prefix_values.astype(jnp.bfloat16)
    attended = jnp.einsum(
        "htu,uhe->hte", local_low, value, preferred_element_type=jnp.float32
    ) + jnp.einsum("htc,hce->hte", cache_low, cache_values, preferred_element_type=jnp.float32)
    delta = jnp.sum(jnp.transpose(dout.astype(jnp.float32), (1, 0, 2)) * attended, axis=-1)[
        ..., None
    ]
    local_grad = jnp.einsum("the,uhe->htu", dout, value, preferred_element_type=jnp.float32)
    local_score_grad = (local_prob * (local_grad - delta) * scale).astype(jnp.bfloat16)
    cache_grad = jnp.einsum("the,hce->htc", dout, cache_values, preferred_element_type=jnp.float32)
    cache_score_grad = (cache_prob * (cache_grad - delta * counts_row) * scale).astype(jnp.bfloat16)
    grad_query = (
        jnp.einsum("htu,uhe->the", local_score_grad, keys, preferred_element_type=jnp.float32)
        + jnp.einsum("htc,hce->the", cache_score_grad, codebook, preferred_element_type=jnp.float32)
    ).astype(jnp.bfloat16)
    key_grad = jnp.einsum(
        "htu,the->uhe", local_score_grad, query, preferred_element_type=jnp.float32
    ).astype(jnp.bfloat16)
    grad_code = jnp.einsum(
        "ths,the->hse", onehot, key_grad, preferred_element_type=jnp.float32
    ) + jnp.einsum("htc,the->hce", cache_score_grad, query, preferred_element_type=jnp.float32)
    value_part = jnp.einsum("htc,the->hce", cache_low, dout, preferred_element_type=jnp.float32)
    local_values = jnp.einsum("htu,the->uhe", local_low, dout, preferred_element_type=jnp.float32)
    return (grad_query, local_values, grad_code, value_part)


def per_device(queries, values, codes, codebook, out_weight, grad_out):
    row_count = queries.shape[0]
    heads_here, entries, head_width = codebook.shape
    weight_columns = lax.all_to_all(out_weight, "head", split_axis=1, concat_axis=0, tiled=True)
    partial_grads = jnp.einsum(
        "tn,hn->th", grad_out, weight_columns, preferred_element_type=jnp.float32
    )
    grad_heads = lax.psum_scatter(partial_grads, "head", scatter_dimension=1, tiled=True)
    grad_heads = grad_heads.astype(jnp.bfloat16).reshape(row_count, heads_here, head_width)
    query_rows = queries.reshape(row_count, heads_here, head_width)
    value_rows = values.reshape(row_count, heads_here, head_width)
    levels = lax.iota(jnp.int32, entries)
    onehot = (codes[:, :, None] == levels[None, None, :]).astype(jnp.bfloat16)
    nblocks = row_count // BLOCK
    spans = [(index * BLOCK, (index + 1) * BLOCK) for index in range(nblocks)]
    own_values = [
        jnp.einsum(
            "ths,the->hse",
            onehot[lower:upper],
            value_rows[lower:upper],
            preferred_element_type=jnp.float32,
        )
        for lower, upper in spans
    ]
    own_counts = [
        jnp.sum(onehot[lower:upper].astype(jnp.float32), axis=0) for lower, upper in spans
    ]
    device_values = reduce(jnp.add, own_values)
    device_counts = reduce(jnp.add, own_counts)
    zero_values = jnp.zeros((heads_here, entries, head_width), jnp.float32)
    zero_counts = jnp.zeros((heads_here, entries), jnp.float32)
    prefix_values, prefix_counts = entering(
        (device_values, device_counts), "seq", add_tree, (zero_values, zero_counts), False
    )
    grad_queries = []
    local_parts = []
    value_parts = []
    code_total = zero_values
    for index in range(nblocks):
        lower, upper = spans[index]
        grad_query, local_values, grad_code, value_part = attend_block(
            query_rows[lower:upper],
            value_rows[lower:upper],
            onehot[lower:upper],
            grad_heads[lower:upper],
            codebook,
            prefix_values,
            prefix_counts,
        )
        grad_queries.append(grad_query)
        local_parts.append(local_values)
        value_parts.append(value_part)
        code_total = code_total + grad_code
        prefix_values = prefix_values + own_values[index]
        prefix_counts = prefix_counts + own_counts[index]
    device_grads = reduce(jnp.add, value_parts)
    later = entering(device_grads, "seq", add_tree, zero_values, True)
    grad_values = [None] * nblocks
    for index in reversed(range(nblocks)):
        lower, upper = spans[index]
        lookup = jnp.einsum(
            "ths,hse->the",
            onehot[lower:upper],
            later.astype(jnp.bfloat16),
            preferred_element_type=jnp.float32,
        )
        grad_values[index] = (local_parts[index] + lookup).astype(jnp.bfloat16)
        later = later + value_parts[index]
    grad_codebook = lax.psum(code_total, "seq")
    grad_query_all = jnp.concatenate(grad_queries, axis=0).reshape(
        row_count, heads_here * head_width
    )
    grad_value_all = jnp.concatenate(grad_values, axis=0).reshape(
        row_count, heads_here * head_width
    )
    return (grad_query_all, grad_value_all, grad_codebook)


def solution(mesh):
    return jax.shard_map(
        per_device,
        mesh=mesh,
        in_specs=(
            P("seq", "head"),
            P("seq", "head"),
            P("seq", "head"),
            P("head", None, None),
            P("head", None),
            P("seq", "head"),
        ),
        out_specs=(P("seq", "head"), P("seq", "head"), P("head", None, None)),
        check_vma=False,
    )
```

profile of v0, /device:TPU:0, one launch (start us, length us, event | category | flops | bytes accessed | tf_op | source)
XLA Modules:
  0.0 398.4 jit_solution(18388749186380675712)
XLA Ops:
  8.1 2.1 fusion.78
  11.2 3.7 fusion.68
  14.9 2.5 copy.261
  17.3 2.3 fusion.16
  20.6 1.9 fusion.18
  22.6 3.9 copy.173
  26.6 29.9 %all_to_all.19 = bf16[512,4,512]{0,2,1:T(8,128)(2,1)S(1)} all-to-all(bf16[512,4,512]{0,2,1:T(8,128)(2,1)} %bitcast.168), channel_id=1, replica_groups=mesh['seq'=8,'head'=4] {'head'}, dimensions={1} | all-to-all | bytes 4194304 | tf_op jit(solution)/shard_map/all_to_all | solution.py:89
  56.5 2.4 copy.174
  58.9 7.3 %fusion.79 = f32[1024,2048]{1,0:T(8,128)} fusion(bf16[1024,512]{1,0:T(8,128)(2,1)S(1)} %copy-done, bf16[2048,512]{1,0:T(8,128)(2,1)} %bitcast.173), kind=kOutput, calls=%fused_computation.113 | convolution fusion | flops 2147483648 | bytes 11534336 | tf_op jit(solution)/shard_map/tn,hn->th/dot_general | solution.py:90
  68.0 3.0 convert_reduce_fusion
  71.1 33.4 %all-gather.3 = f32[8,4,512]{2,1,0:T(4,128)S(1)} all-gather(f32[1,4,512]{2,1,0:T(4,128)S(1)} %add_bitcast_fusion), channel_id=3, replica_groups=mesh['seq'=8,'head'=4] {'seq'}, dimensions={0}, use_global_device_ids=true | all-gather | bytes 73728 | tf_op jit(solution)/shard_map/all_gather | solution.py:13
  106.9 2.0 copy-done.2
  108.9 3.2 fusion.4
  112.2 38.8 %all-gather.7.cloned.1.call-done = f32[32,512,128]{2,1,0:T(8,128)} async-done(((f32[4,512,128]{2,1,0:T(8,128)}), f32[32,512,128]{2,1,0:T(8,128)}) %all-gather.7.cloned.1.call-update) | async-done | bytes 8388624 | tf_op jit(solution)/shard_map/all_gather | solution.py:13
  151.0 12.9 %while.32 = (s32[]{:T(128)}, f32[4,512,128]{2,1,0:T(8,128)S(1)}, f32[4,512]{1,0:T(4,128)S(1)}, s32[]{:T(128)}, f32[8,4,512,128]{3,2,1,0:T(8,128)}, /*index=5*/f32[8,4,512]{2,1,0:T(4,128)S(1)}, s32[]{:T(128)}, s32[]{:T(128)}) while((s32[]{:T(128)}, f32[4,512,128]{2,1,0:T(8,128)S(1)}, f32[4,512]{1,0:T(4,128)S(1)}, s32[]{:T(128)}, ...), condition=%wide.region_4.5_spmd.clone, body=%wide.region_3.4_spmd.clone.sunk | while | flops 792580 | bytes 3170427 | solution.py:26
  154.2 1.6 add_select_fusion.6
  155.8 1.6 add_select_fusion.6
  157.4 1.6 add_select_fusion.6
  159.1 1.6 add_select_fusion.6
  160.7 1.6 add_select_fusion.6
  166.5 3.7 copy-done.5
  170.2 5.5 %fusion.11 = (f32[4,512]{1,0:T(4,128)S(1)}, f32[4,512]{1,0:T(4,128)S(1)}, f32[4,512]{1,0:T(4,128)S(1)}, f32[4,512]{1,0:T(4,128)S(1)}) fusion(f32[4,512,512]{2,1,0:T(8,128)S(1)} %copy-done.5, f32[4,512]{1,0:T(4,128)S(1)} %max.16, pred[512,512]{0,1:T(8,128)(4,1)S(1)} %iota_compare_fusion.1, f32[4,512]{1,0:T(4,128)S(1)} %max.17, ...), kind=kLoop, calls=%fused_computation.31 | loop fusion | flops 23060480 | bytes 17108992 | tf_op jit(solution)/shard_map/reduce_sum | solution.py:53
  175.8 1.7 convert_element_type.97
  179.7 3.4 fusion.46
  183.4 2.4 convolution_add_fusion.6
  187.5 4.4 %fusion.48 = f32[4,512,128]{1,2,0:T(8,128)} fusion(bf16[4,512,128]{2,1,0:T(8,128)(2,1)S(1)} %add_convert_fusion.1, f32[4,512,512]{1,2,0:T(8,128)} %copy-done.12, f32[4,512]{1,0:T(4,128)S(1)} %add.160, f32[4,512]{1,0:T(4,128)S(1)} %max.17, pred[4,512]{1,0:T(4,128)(4,1)S(1)} %get-tuple-element.302), kind=kOutput, calls=%fused_computation.85 | convolution fusion | flops 274726912 | bytes 5785600 | tf_op jit(solution)/shard_map/htc,hce->hte/dot_general | solution.py:63
  191.8 2.3 fusion.54
  194.2 2.1 copy.277
  196.2 4.5 %fusion.31 = f32[4,512]{1,0:T(4,128)S(1)} fusion(f32[4,512,128]{1,2,0:T(8,128)} %fusion.48, bf16[512,4,128]{0,2,1:T(8,128)(2,1)} %bitcast.177, bf16[512,4,128]{0,2,1:T(8,128)(2,1)} %bitcast.181, f32[4,512,512]{2,1,0:T(8,128)} %copy-done.2, f32[4,512]{1,0:T(4,128)S(1)} %add.160, f32[4,512]{1,0:T(4,128)S(1)} %max.17, pred[512,512]{0,1:T(8,128)(4,1)S(1)} %iota_compare_fusion.1), kind=kOutput, calls=%fused_computation.64 | convolution fusion | flops 275773440 | bytes 6578176 | tf_op jit(solution)/shard_map/htu,uhe->hte/dot_general | solution.py:61
  200.8 2.0 multiply_convert_fusion
  204.2 1.6 fusion.30
  206.5 2.2 multiply_convert_fusion.2
  209.3 1.9 multiply_convert_fusion.1
  211.8 1.9 multiply_convert_fusion.3
  215.2 1.6 copy.219
  216.7 3.3 fusion.81
  220.0 2.3 fusion.82
  222.3 4.5 %convolution_add_fusion.1 = f32[4,512,128]{2,1,0:T(8,128)} fusion(f32[4,512,128]{2,1,0:T(8,128)} %fusion.81, bf16[4,512,512]{1,2,0:T(8,128)(2,1)} %copy-done.23, bf16[512,4,128]{0,2,1:T(8,128)(2,1)S(1)} %bitcast.166, pred[1024,4,512]{2,0,1:T(32,128)(4,1)} %copy-done.19), kind=kOutput, calls=%fused_computation.45 | convolution fusion | flops 537395200 | bytes 5767168 | tf_op jit(solution)/shard_map/ths,the->hse/dot_general | solution.py:78
  226.8 4.6 %fusion.21 = f32[4,512,128]{2,1,0:T(8,128)} fusion(f32[4,512,128]{2,1,0:T(8,128)} %convolution_add_fusion.1, f32[4,512,128]{2,1,0:T(8,128)S(1)} %fusion.82, bf16[4,512,512]{1,2,0:T(8,128)(2,1)} %copy-done.22, bf16[512,4,128]{0,2,1:T(8,128)(2,1)S(1)} %bitcast.162, pred[1024,4,512]{2,0,1:T(32,128)(4,1)} %copy-done.19), kind=kOutput, calls=%fused_computation.44 | convolution fusion | flops 537657344 | bytes 6815744 | tf_op jit(solution)/shard_map/ths,the->hse/dot_general | solution.py:78
  231.4 4.8 %fusion.50 = f32[4,128,512]{2,1,0:T(8,128)} fusion(bf16[512,4,128]{0,2,1:T(8,128)(2,1)S(1)} %bitcast.184, f32[4,512,512]{2,1,0:T(8,128)} %copy-done.2, f32[4,512]{1,0:T(4,128)S(1)} %add.160, f32[4,512]{1,0:T(4,128)S(1)} %max.17, pred[512,512]{0,1:T(8,128)(4,1)S(1)} %iota_compare_fusion.1), kind=kOutput, calls=%fused_computation.87 | convolution fusion | flops 274726912 | bytes 6045696 | tf_op jit(solution)/shard_map/htu,the->uhe/dot_general | solution.py:82
  237.9 70.8 %all-gather.9.cloned.1.call-done = f32[32,512,128]{2,1,0:T(8,128)} async-done(((f32[4,512,128]{2,1,0:T(8,128)}), f32[32,512,128]{2,1,0:T(8,128)}) %all-gather.9.cloned.1.call-update) | async-done | bytes 8388624 | tf_op jit(solution)/shard_map/all_gather | solution.py:13
  308.6 12.9 %while.33 = (s32[]{:T(128)}, f32[4,512,128]{2,1,0:T(8,128)S(1)}, s32[]{:T(128)}, f32[8,4,512,128]{3,2,1,0:T(8,128)}, s32[]{:T(128)}, /*index=5*/s32[]{:T(128)}, s32[]{:T(128)}, s32[]{:T(128)}) while((s32[]{:T(128)}, f32[4,512,128]{2,1,0:T(8,128)S(1)}, s32[]{:T(128)}, f32[8,4,512,128]{3,2,1,0:T(8,128)}, s32[]{:T(128)}, ...), condition=%wide.region_16.17_spmd.clone, body=%wide.region_15.16_spmd.clone.sunk | while | flops 786440 | bytes 3145891 | solution.py:26
  308.6 1.7 add_select_fusion.8
  315.1 1.7 add_select_fusion.8
  320.0 1.6 add_select_fusion.8
  321.6 2.2 fusion.36
  326.2 62.3 %all-reduce.2.cloned.1.call-done = f32[4,512,128]{2,1,0:T(8,128)} async-done(((f32[4,512,128]{2,1,0:T(8,128)}), f32[4,512,128]{2,1,0:T(8,128)}) %all-reduce.2.cloned.1.call-update) | async-done | bytes 1048592 | tf_op jit(solution)/shard_map/psum | solution.py:154
  388.6 2.3 copy.295
  (142 shorter events, 34.2 us)
Async XLA Ops:
  8.0 50.9 %copy-start = (bf16[1024,512]{1,0:T(8,128)(2,1)S(1)}, bf16[1024,512]{1,0:T(8,128)(2,1)}, u32[]{:S(2)}) copy-start(bf16[1024,512]{1,0:T(8,128)(2,1)} %param.15) | copy-start | bytes 3145732
  8.0 143.0 %all-gather.7.cloned.1.call-start = ((), (), s32[]{:S(2)}) async-start(), calls=%async_computation.4 | async-start | bytes 9437184 | tf_op jit(solution)/shard_map/all_gather | solution.py:13
  14.9 7.7 %copy-start.19 = (pred[1024,4,512]{2,0,1:T(32,128)(4,1)}, pred[1024,4,512]{2,0,1:T(32,128)(4,1)S(1)}, u32[]{:S(2)}) copy-start(pred[1024,4,512]{2,0,1:T(32,128)(4,1)S(1)} %get-tuple-element.312) | copy-start | bytes 6291460
  17.3 3.3 copy-start.36
  19.6 1.0 copy-start.28
  22.6 153.2 %reduce-scatter.2.cloned.1.call-start = ((), (), s32[]{:S(2)}) async-start(), calls=%async_computation.2 | async-start | bytes 10485760 | tf_op jit(solution)/shard_map/reduce_scatter | solution.py:93
  66.2 242.5 %all-gather.9.cloned.1.call-start = ((), (), s32[]{:S(2)}) async-start(), calls=%async_computation.5 | async-start | bytes 9437184 | tf_op jit(solution)/shard_map/all_gather | solution.py:13
  66.2 38.3 %copy-start.14 = (bf16[4,512,128]{2,1,0:T(8,128)(2,1)S(1)}, bf16[4,512,128]{2,1,0:T(8,128)(2,1)}, u32[]{:S(2)}) copy-start(bf16[4,512,128]{2,1,0:T(8,128)(2,1)} %param.13) | copy-start | bytes 1572868
  68.0 95.9 %copy-start.15 = (bf16[512,512]{0,1:T(8,128)(2,1)}, bf16[512,512]{0,1:T(8,128)(2,1)S(1)}, u32[]{:S(2)}) copy-start(bf16[512,512]{0,1:T(8,128)(2,1)S(1)} %copy.259) | copy-start | bytes 1572868
  68.0 36.5 %copy-start.20 = (pred[1024,4,512]{2,0,1:T(32,128)(4,1)S(1)}, pred[1024,4,512]{2,0,1:T(32,128)(4,1)}, u32[]{:S(2)}) copy-start(pred[1024,4,512]{2,0,1:T(32,128)(4,1)} %copy-done.19) | copy-start | bytes 6291460
  105.4 1.5 copy-start.26
  106.2 6.0 %copy-start.24 = (bf16[512,4,128]{2,0,1:T(8,128)(2,1)}, bf16[512,4,128]{2,0,1:T(8,128)(2,1)S(1)}, u32[]{:S(2)}) copy-start(bf16[512,4,128]{2,0,1:T(8,128)(2,1)S(1)} %fusion.32) | copy-start | bytes 1572868
  106.9 2.0 copy-start.2
  163.9 2.6 copy-start.3
  163.9 6.3 %copy-start.5 = (f32[4,512,512]{2,1,0:T(8,128)S(1)}, f32[4,512,512]{2,1,0:T(8,128)}, u32[]{:S(2)}) copy-start(f32[4,512,512]{2,1,0:T(8,128)} %get-tuple-element.314) | copy-start | bytes 12582916
  165.2 10.5 %copy-start.8 = (f32[4,512,512]{1,2,0:T(8,128)}, f32[4,512,512]{1,2,0:T(8,128)S(1)}, u32[]{:S(2)}) copy-start(f32[4,512,512]{1,2,0:T(8,128)S(1)} %get-tuple-element.316) | copy-start | bytes 12582916
  166.5 9.3 %copy-start.12 = (f32[4,512,512]{1,2,0:T(8,128)}, f32[4,512,512]{1,2,0:T(8,128)S(1)}, u32[]{:S(2)}) copy-start(f32[4,512,512]{1,2,0:T(8,128)S(1)} %get-tuple-element.318) | copy-start | bytes 12582916
  179.7 3.6 copy-start.9
  179.7 3.7 copy-start.31
  183.1 2.7 copy-start.29
  185.8 202.7 %all-reduce.2.cloned.1.call-start = ((), (), s32[]{:S(2)}) async-start(), calls=%async_computation.3 | async-start | bytes 2097152 | tf_op jit(solution)/shard_map/psum | solution.py:154
  187.4 4.4 %copy-start.33 = (bf16[4,512,128]{2,1,0:T(8,128)(2,1)}, bf16[4,512,128]{2,1,0:T(8,128)(2,1)S(1)}, u32[]{:S(2)}) copy-start(bf16[4,512,128]{2,1,0:T(8,128)(2,1)S(1)} %add_convert_fusion.1) | copy-start | bytes 1572868
  187.4 4.4 %copy-start.10 = (f32[4,512,512]{1,2,0:T(8,128)S(1)}, f32[4,512,512]{1,2,0:T(8,128)}, u32[]{:S(2)}) copy-start(f32[4,512,512]{1,2,0:T(8,128)} %copy-done.8) | copy-start | bytes 12582916
  196.2 4.5 %copy-start.13 = (f32[4,512,512]{1,2,0:T(8,128)S(1)}, f32[4,512,512]{1,2,0:T(8,128)}, u32[]{:S(2)}) copy-start(f32[4,512,512]{1,2,0:T(8,128)} %copy-done.12) | copy-start | bytes 12582916
  196.2 4.5 %copy-start.34 = (bf16[4,512,128]{2,1,0:T(8,128)(2,1)S(1)}, bf16[4,512,128]{2,1,0:T(8,128)(2,1)}, u32[]{:S(2)}) copy-start(bf16[4,512,128]{2,1,0:T(8,128)(2,1)} %copy-done.33) | copy-start | bytes 1572868
  196.2 4.5 %copy-start.38 = (bf16[512,512]{0,1:T(8,128)(2,1)S(1)}, bf16[512,512]{0,1:T(8,128)(2,1)}, u32[]{:S(2)}) copy-start(bf16[512,512]{0,1:T(8,128)(2,1)} %copy.263) | copy-start | bytes 1572868
  200.8 3.4 copy-start.6
  200.8 3.4 copy-start.35
  200.8 3.4 copy-start.40
  200.8 3.4 copy-start.43
  202.8 1.3 copy-start.17
  204.2 2.2 copy-start.11
  204.2 2.3 copy-start.32
  206.5 2.8 copy-start.4
  206.5 2.8 copy-start.37
  208.7 2.5 copy-start.18
  209.3 1.9 copy-start.27
  211.2 2.5 copy-start.22
  211.8 1.9 copy-start.25
  213.7 1.3 copy-start.23
  213.7 3.0 copy-start.16
  226.8 4.6 %copy-start.39 = (bf16[512,512]{0,1:T(8,128)(2,1)S(1)}, bf16[512,512]{0,1:T(8,128)(2,1)}, u32[]{:S(2)}) copy-start(bf16[512,512]{0,1:T(8,128)(2,1)} %copy.263) | copy-start | bytes 1572868
  231.4 4.8 %copy-start.7 = (f32[4,512,512]{2,1,0:T(8,128)S(1)}, f32[4,512,512]{2,1,0:T(8,128)}, u32[]{:S(2)}) copy-start(f32[4,512,512]{2,1,0:T(8,128)} %get-tuple-element.314) | copy-start | bytes 12582916
  231.4 4.8 %copy-start.41 = (bf16[512,512]{0,1:T(8,128)(2,1)S(1)}, bf16[512,512]{0,1:T(8,128)(2,1)}, u32[]{:S(2)}) copy-start(bf16[512,512]{0,1:T(8,128)(2,1)} %copy.277) | copy-start | bytes 1572868
  308.6 13.0 %copy-start.42 = (f32[4,128,512]{2,1,0:T(8,128)S(1)}, f32[4,128,512]{2,1,0:T(8,128)}, u32[]{:S(2)}) copy-start(f32[4,128,512]{2,1,0:T(8,128)} %fusion.50) | copy-start | bytes 3145732
  321.6 2.2 copy-start.21
  321.6 2.2 copy-start.30
  323.8 67.0 %copy-start.1 = (bf16[1024,512]{1,0:T(8,128)(2,1)S(1)}, bf16[1024,512]{1,0:T(8,128)(2,1)}, u32[]{:S(2)}) copy-start(bf16[1024,512]{1,0:T(8,128)(2,1)} %param.15) | copy-start | bytes 3145732
Sparse Core Ops, SparseCore 0:
  22.7 128.2 all-gather.6
  185.9 122.6 all-gather.8
  312.1 76.3 all-reduce.1
Sparse Core Ops, SparseCore 1:
  66.2 72.2 reduce-scatter.1
where the time goes:
time: 405 us; the launch traced here: 398 us
  waiting for transfers between devices  172 us (42%)
  matrix products  72.4 us (18%)
  blocking collectives  63.3 us (16%)
  other arithmetic  41 us (10%)
  local copies, waits for them, and re-layouts  32.5 us (8%)
  between operations  16.3 us (4%)
    all_gather x2, waiting for transfers between devices, entering(): everything = jax.tree.map(lambda part: lax.all_gather(part, axis), array)  110 us
    psum x1, waiting for transfers between devices, per_device(): grad_codebook = lax.psum(code_total, 'seq')  62.3 us
    all_gather x1, blocking collectives, entering(): everything = jax.tree.map(lambda part: lax.all_gather(part, axis), array)  33.4 us
    all_to_all x1, blocking collectives, per_device(): lax.all_to_all(out_weight, 'head', split_axis=1, concat_axis=0, tiled=True)  29.9 us
    select_n x24, other arithmetic, hop(): return jax.tree.map(lambda a, b: jnp.where(reached, a, b), new, before)  25.4 us
    unnamed x97, local copies, waits for them, and re-layouts  23.6 us
    dot_general x2, matrix products, attend_block(): jnp.einsum('ths,the->hse', onehot, key_grad, preferred_element_type=jnp.f...  9.12 us
  transfers between devices with their start and end apart: 4, of which 3 were waited for; matrix products, arithmetic and copies ran while one was open for 28% of the time, Pallas kernels for 0%

commit v1 on v0

v1 whole, which is shorter than its diff:
```python
import functools

import jax
import jax.numpy as jnp
from jax import lax
from jax.experimental import pallas as pl
from jax.experimental.pallas import tpu as pltpu
from jax.sharding import PartitionSpec as P

BLOCK = 512
CHUNKS = 4
NEG = -1e30
F32 = jnp.float32
BF16 = jnp.bfloat16
MESH = pl.DeviceIdType.MESH


def nn(a, b):
    return lax.dot_general(a, b, (((1,), (0,)), ((), ())), preferred_element_type=F32)


def nt(a, b):
    return lax.dot_general(a, b, (((1,), (1,)), ((), ())), preferred_element_type=F32)


def kernel(
    n_seq, n_head,
    q_ref, v_ref, codes_ref, cb_ref, w_ref, go_ref,
    gq_ref, gv_ref, gc_ref,
    gath, dout, hot_t, hot, keys, keys_t, own, cnt_block, cnt_send, cnt_recv, cnt_before,
    p1_send, p1_recv, p2_send, p2_recv, local_part, vpart, s1_send, s1_recv, s2_send, s2_recv,
    ag_s, ag_r, cn_s, cn_r, p1_s, p1_r, p2_s, p2_r, s1_s, s1_r, s2_s, s2_r,
):
    rows_all = q_ref.shape[0]
    heads, entries, width = cb_ref.shape
    nb = rows_all // BLOCK
    part = entries // n_seq
    scale = width ** (-0.5)
    me = lax.axis_index("seq")
    mine = lax.axis_index("head")
    bits = []
    bit = n_head // 2
    while bit >= 1:
        bits.append(bit)
        bit //= 2

    def flip(index, mask):
        for b in bits:
            if mask & b:
                index = index + b - 2 * b * ((index // b) % 2)
        return index

    barrier = pltpu.get_barrier_semaphore()

    def greet(k, carry):
        pl.semaphore_signal(barrier, inc=1, device_id={"seq": (me + k) % n_seq}, device_id_type=MESH)
        return carry

    lax.fori_loop(1, n_seq, greet, 0)
    for b in bits:
        pl.semaphore_signal(barrier, inc=1, device_id={"head": flip(mine, b)}, device_id_type=MESH)
    pl.semaphore_wait(barrier, n_seq - 1 + len(bits))

    piece = rows_all // CHUNKS

    def gather_copy(src_mask, to, chunk):
        block = flip(mine, src_mask)
        span = pl.ds(chunk * piece, piece)
        src = go_ref.at[span] if src_mask == 0 else gath.at[block, span]
        slot = src_mask ^ to
        return pltpu.make_async_remote_copy(
            src_ref=src, dst_ref=gath.at[block, span],
            send_sem=ag_s.at[slot, chunk], recv_sem=ag_r.at[slot, chunk],
            device_id={"head": flip(mine, to)}, device_id_type=MESH)

    plan = []
    known = [0]
    for b in bits:
        plan += [(m, b) for m in known]
        known += [m ^ b for m in known]
    for m, b in plan:
        if m == 0:
            for chunk in range(CHUNKS):
                gather_copy(m, b, chunk).start()
    by_slot = {m ^ b: (m, b) for m, b in plan}
    taken = set()

    def arrive(slot, chunk):
        if (slot, chunk) not in taken:
            taken.add((slot, chunk))
            m, b = by_slot[slot]
            gather_copy(m, b, chunk).wait_recv()

    def forward(chunk):
        for m, b in plan:
            if m != 0:
                arrive(m, chunk)
                gather_copy(m, b, chunk).start()

    gath[mine] = go_ref[...]

    row_at = lax.broadcasted_iota(jnp.int32, (entries, BLOCK), 0)
    lane_at = lax.broadcasted_iota(jnp.int32, (BLOCK, entries), 1)

    def sums(h, carry):
        head_lanes = pl.ds(pl.multiple_of(h * width, width), width)
        total_values = jnp.zeros((entries, width), F32)
        total_counts = jnp.zeros((1, entries), F32)
        for b in range(nb):
            rows = pl.ds(b * BLOCK, BLOCK)
            code_row = codes_ref[h, :, rows]
            code_full = jnp.transpose(jnp.broadcast_to(code_row, (width, BLOCK)))
            code_cols = jnp.concatenate([code_full] * (entries // width), axis=1)
            one_t = (row_at == code_row).astype(F32).astype(BF16)
            one_f = (lane_at == code_cols).astype(F32)
            one = one_f.astype(BF16)
            hot_t[h, b] = one_t
            hot[h, b] = one
            key = nn(one, cb_ref[h])
            keys[h, b] = key.astype(BF16)
            keys_t[h, b] = jnp.transpose(key).astype(BF16)
            values = nn(one_t, v_ref[rows, head_lanes])
            counts = jnp.sum(one_f, axis=0, keepdims=True)
            own[h, b] = values
            cnt_block[h, b] = counts
            total_values += values
            total_counts += counts
        p1_send[:, h] = total_values.astype(BF16).reshape(n_seq, part, width)
        cnt_send[h] = total_counts
        return carry

    lax.fori_loop(0, heads, sums, 0)

    def count_copy(to, source):
        return pltpu.make_async_remote_copy(
            src_ref=cnt_send, dst_ref=cnt_recv.at[source], send_sem=cn_s.at[to], recv_sem=cn_r.at[source],
            device_id={"seq": to}, device_id_type=MESH)

    def prefix_out(to, source):
        return pltpu.make_async_remote_copy(
            src_ref=p1_send.at[to], dst_ref=p1_recv.at[source], send_sem=p1_s.at[to], recv_sem=p1_r.at[source],
            device_id={"seq": to}, device_id_type=MESH)

    def prefix_back(to, source):
        return pltpu.make_async_remote_copy(
            src_ref=p2_send.at[to], dst_ref=p2_recv.at[source], send_sem=p2_s.at[to], recv_sem=p2_r.at[source],
            device_id={"seq": to}, device_id_type=MESH)

    def over_peers(action):
        def body(k, carry):
            action((me + k) % n_seq)
            return carry

        lax.fori_loop(1, n_seq, body, 0)

    def send_sums(peer):
        prefix_out(peer, me).start()
        count_copy(peer, me).start()

    over_peers(send_sums)
    p1_recv[me] = p1_send[me]
    for chunk in range(CHUNKS // 2):
        forward(chunk)
    over_peers(lambda peer: prefix_out(peer, peer).wait_recv())

    def scan_step(j, total):
        p2_send[j] = total.astype(BF16)
        return total + p1_recv[j].astype(F32)

    lax.fori_loop(0, n_seq, scan_step, jnp.zeros((heads, part, width), F32))
    over_peers(lambda peer: prefix_back(peer, me).start())
    p2_recv[me] = p2_send[me]
    over_peers(lambda peer: count_copy(peer, peer).wait_recv())
    cnt_before[...] = lax.fori_loop(0, me, lambda j, total: total + cnt_recv[j], jnp.zeros(cnt_before.shape, F32))
    for chunk in range(CHUNKS // 2, CHUNKS):
        forward(chunk)
    for chunk in range(CHUNKS):
        for slot in by_slot:
            arrive(slot, chunk)

    depth = go_ref.shape[1]

    def project(r, carry):
        rows = pl.ds(pl.multiple_of(r * BLOCK, BLOCK), BLOCK)
        total = nt(gath[0, rows], w_ref[:, 0:depth])
        for k in range(1, n_head):
            total += nt(gath[k, rows], w_ref[:, k * depth:(k + 1) * depth])
        dout[rows] = total.astype(BF16)
        return carry

    lax.fori_loop(0, nb, project, 0)
    over_peers(lambda peer: prefix_back(peer, peer).wait_recv())

    def late_out(h, to, source):
        return pltpu.make_async_remote_copy(
            src_ref=s1_send.at[h, to], dst_ref=s1_recv.at[h, source],
            send_sem=s1_s.at[h, to], recv_sem=s1_r.at[h, source],
            device_id={"seq": to}, device_id_type=MESH)

    def late_back(h, to, source):
        return pltpu.make_async_remote_copy(
            src_ref=s2_send.at[h, to], dst_ref=s2_recv.at[h, source],
            send_sem=s2_s.at[h, to], recv_sem=s2_r.at[h, source],
            device_id={"seq": to}, device_id_type=MESH)

    def combine(h):
        over_peers(lambda peer: late_out(h, peer, peer).wait_recv())

        def code_step(j, total):
            return total + s1_recv[h, j, 1].astype(F32)

        code = lax.fori_loop(0, n_seq, code_step, jnp.zeros((part, width), F32)).astype(BF16)

        def later_step(k, total):
            j = n_seq - 1 - k
            s2_send[h, j, 0] = total.astype(BF16)
            s2_send[h, j, 1] = code
            return total + s1_recv[h, j, 0].astype(F32)

        lax.fori_loop(0, n_seq, later_step, jnp.zeros((part, width), F32))
        over_peers(lambda peer: late_back(h, peer, me).start())
        s2_recv[h, me] = s2_send[h, me]

    def attend(h, carry):
        head_lanes = pl.ds(pl.multiple_of(h * width, width), width)
        book = cb_ref[h]
        book_t = jnp.transpose(book.astype(F32)).astype(BF16)
        prefix = p2_recv[:, h].astype(F32).reshape(entries, width)
        count_row = cnt_before[h]
        code_total = jnp.zeros((entries, width), F32)
        part_total = jnp.zeros((entries, width), F32)
        for b in range(nb):
            rows = pl.ds(b * BLOCK, BLOCK)
            query = q_ref[rows, head_lanes]
            value = v_ref[rows, head_lanes]
            grad = dout[rows, head_lanes]
            key = keys[h, b]
            cache_values = prefix.astype(BF16)
            count_full = jnp.transpose(jnp.broadcast_to(count_row, (width, entries)))
            bias_full = jnp.where(count_full > 0.0, 0.0, NEG)
            counts = jnp.concatenate([count_full] * (BLOCK // width), axis=1)
            bias = jnp.concatenate([bias_full] * (BLOCK // width), axis=1)
            at_u = lax.broadcasted_iota(jnp.int32, (BLOCK, BLOCK), 0)
            at_t = lax.broadcasted_iota(jnp.int32, (BLOCK, BLOCK), 1)
            scores = jnp.where(at_u <= at_t, nt(key, query) * scale, NEG)
            cache_scores = nt(book, query) * scale + bias
            highest = jnp.maximum(
                jnp.max(scores, axis=0, keepdims=True), jnp.max(cache_scores, axis=0, keepdims=True))
            local_exp = jnp.exp(scores - highest)
            cache_exp = jnp.exp(cache_scores - highest)
            total = jnp.sum(local_exp, axis=0, keepdims=True) + jnp.sum(cache_exp * counts, axis=0, keepdims=True)
            inverse = 1.0 / total
            local_prob = local_exp * inverse
            cache_prob = cache_exp * inverse
            local_low = local_prob.astype(BF16)
            cache_low = cache_prob.astype(BF16)
            local_grad = nt(value, grad)
            cache_grad = nt(cache_values, grad)
            delta = (jnp.sum(local_low.astype(F32) * local_grad, axis=0, keepdims=True)
                     + jnp.sum(cache_low.astype(F32) * cache_grad, axis=0, keepdims=True))
            local_score_grad = (local_prob * (local_grad - delta) * scale).astype(BF16)
            cache_score_grad = (cache_prob * (cache_grad - delta * counts) * scale).astype(BF16)
            gq_t = nn(keys_t[h, b], local_score_grad) + nn(book_t, cache_score_grad)
            gq_ref[rows, head_lanes] = jnp.transpose(gq_t).astype(BF16)
            key_grad = nn(local_score_grad, query).astype(BF16)
            code_total += nn(hot_t[h, b], key_grad) + nn(cache_score_grad, query)
            value_part = nn(cache_low, grad)
            vpart[h, b] = value_part
            part_total += value_part
            local_part[h, b] = nn(local_low, grad)
            prefix = prefix + own[h, b]
            count_row = count_row + cnt_block[h, b]
        s1_send[h, :, 0] = part_total.astype(BF16).reshape(n_seq, part, width)
        s1_send[h, :, 1] = code_total.astype(BF16).reshape(n_seq, part, width)
        s1_recv[h, me] = s1_send[h, me]
        over_peers(lambda peer: late_out(h, peer, me).start())

        @pl.when(h >= 1)
        def _():
            combine(h - 1)

        return carry

    lax.fori_loop(0, heads, attend, 0)
    combine(heads - 1)

    def finish(h, carry):
        head_lanes = pl.ds(pl.multiple_of(h * width, width), width)
        over_peers(lambda peer: late_back(h, peer, peer).wait_recv())
        gc_ref[h] = s2_recv[h, :, 1].astype(F32).reshape(entries, width)
        later = s2_recv[h, :, 0].astype(F32).reshape(entries, width)
        for b in reversed(range(nb)):
            rows = pl.ds(b * BLOCK, BLOCK)
            lookup = nn(hot[h, b], later.astype(BF16))
            gv_ref[rows, head_lanes] = (local_part[h, b] + lookup).astype(BF16)
            later = later + vpart[h, b]
        over_peers(lambda peer: late_out(h, peer, me).wait_send())
        over_peers(lambda peer: late_back(h, peer, me).wait_send())
        return carry

    lax.fori_loop(0, heads, finish, 0)

    def drain(peer):
        prefix_out(peer, me).wait_send()
        prefix_back(peer, me).wait_send()
        count_copy(peer, me).wait_send()

    over_peers(drain)
    for m, b in plan:
        for chunk in range(CHUNKS):
            gather_copy(m, b, chunk).wait_send()


def per_device(queries, values, codes, codebook, out_weight, grad_out):
    n_seq, n_head = lax.axis_size("seq"), lax.axis_size("head")
    row_count = queries.shape[0]
    heads, entries, width = codebook.shape
    nb = row_count // BLOCK
    part = entries // n_seq
    codes_t = codes.T.reshape(heads, 1, row_count)
    vmem = pl.BlockSpec(memory_space=pltpu.VMEM)
    dma = pltpu.SemaphoreType.DMA
    late = pltpu.VMEM((heads, n_seq, 2, part, width), BF16)
    early = pltpu.VMEM((n_seq, heads, part, width), BF16)
    return pl.pallas_call(
        functools.partial(kernel, n_seq, n_head),
        out_shape=(
            jax.ShapeDtypeStruct(queries.shape, BF16),
            jax.ShapeDtypeStruct(queries.shape, BF16),
            jax.ShapeDtypeStruct(codebook.shape, F32),
        ),
        in_specs=[vmem] * 6,
        out_specs=(vmem,) * 3,
        scratch_shapes=[
            pltpu.VMEM((n_head,) + grad_out.shape, BF16),
            pltpu.VMEM(queries.shape, BF16),
            pltpu.VMEM((heads, nb, entries, BLOCK), BF16),
            pltpu.VMEM((heads, nb, BLOCK, entries), BF16),
            pltpu.VMEM((heads, nb, BLOCK, width), BF16),
            pltpu.VMEM((heads, nb, width, BLOCK), BF16),
            pltpu.VMEM((heads, nb, entries, width), F32),
            pltpu.VMEM((heads, nb, 1, entries), F32),
            pltpu.VMEM((heads, 1, entries), F32),
            pltpu.VMEM((n_seq, heads, 1, entries), F32),
            pltpu.VMEM((heads, 1, entries), F32),
            early, early, early, early,
            pltpu.VMEM((heads, nb, BLOCK, width), F32),
            pltpu.VMEM((heads, nb, entries, width), F32),
            late, late, late, late,
            dma((n_head, CHUNKS)), dma((n_head, CHUNKS)),
            dma((n_seq,)), dma((n_seq,)),
            dma((n_seq,)), dma((n_seq,)),
            dma((n_seq,)), dma((n_seq,)),
            dma((heads, n_seq)), dma((heads, n_seq)),
            dma((heads, n_seq)), dma((heads, n_seq)),
        ],
        compiler_params=pltpu.CompilerParams(
            collective_id=0, has_side_effects=True, vmem_limit_bytes=60 * 1024 * 1024),
    )(queries, values, codes_t, codebook, out_weight, grad_out)


def solution(mesh):
    return jax.shard_map(
        per_device,
        mesh=mesh,
        in_specs=(
            P("seq", "head"),
            P("seq", "head"),
            P("seq", "head"),
            P("head", None, None),
            P("head", None),
            P("seq", "head"),
        ),
        out_specs=(P("seq", "head"), P("seq", "head"), P("head", None, None)),
        check_vma=False,
    )
```

time: 405 us -> 99.9 us (0.25); the launches traced: 398 us -> 99.6 us
  waiting for transfers between devices: 172 us -> 0 us
  Pallas kernels: 0 us -> 93.3 us
  matrix products: 72.4 us -> 0 us
  blocking collectives: 63.3 us -> 0 us
  other arithmetic: 41 us -> 0 us
  local copies, waits for them, and re-layouts: 32.5 us -> 5.69 us
  between operations: 16.3 us -> 0.66 us
    all_gather x2 -> x0, waiting for transfers between devices: 110 us -> none  [entering(): everything = jax.tree.map(lambda part: lax.all_gather(part, axis), array)]
    pallas_call x0 -> x1, Pallas kernels: none -> 93.3 us  [per_device(): pl.pallas_call(functools.partial(kernel, n_seq, n_head), out_shape=(jax.S...]
    dot_general x31 -> x0, matrix products: 72.4 us -> none  [the longest x2 9.12 us: attend_block(): jnp.einsum('ths,the->hse', onehot, key_grad, preferred_element_type=jnp.f...]
    psum x1 -> x0, waiting for transfers between devices: 62.3 us -> none  [per_device(): grad_codebook = lax.psum(code_total, 'seq')]
    all_gather x1 -> x0, blocking collectives: 33.4 us -> none  [entering(): everything = jax.tree.map(lambda part: lax.all_gather(part, axis), array)]
    all_to_all x1 -> x0, blocking collectives: 29.9 us -> none  [per_device(): lax.all_to_all(out_weight, 'head', split_axis=1, concat_axis=0, tiled=True)]
    select_n x24 -> x0, other arithmetic: 25.4 us -> none  [hop(): return jax.tree.map(lambda a, b: jnp.where(reached, a, b), new, before)]
    unnamed x97 -> x7, local copies, waits for them, and re-layouts: 23.6 us -> 4.36 us
  transfers between devices with their start and end apart: 4 -> 0, of which waited for: 3 -> 0; matrix products, arithmetic and copies ran while one was open for 28% -> 0% of each run, Pallas kernels for 0% -> 0%
where the time goes in v1:
time: 99.9 us; the launch traced here: 99.6 us
  Pallas kernels  93.3 us (93%)
  local copies, waits for them, and re-layouts  5.69 us (6%)
    pallas_call x1, Pallas kernels, per_device(): pl.pallas_call(functools.partial(kernel, n_seq, n_head), out_shape=(jax.S...  93.3 us
    unnamed x7, local copies, waits for them, and re-layouts  4.36 us

profile of v1, /device:TPU:0, one launch (start us, length us, event | category | flops | bytes accessed | tf_op | source)
XLA Modules:
  0.0 99.6 jit_solution(1526587193798404922)
XLA Ops:
  0.6 1.3 %reshape.9.codes_ref = s32[4,1,1024]{2,1,0:T(1,128)} reshape(s32[4,1024]{1,0:T(4,128)} %bitcast.1) | data formatting | bytes 32768 | tf_op jit(solution)/shard_map/reshape | solution.py:320
  2.0 93.3 %shard_map.85 = (bf16[1024,512]{1,0:T(8,128)(2,1)}, bf16[1024,512]{1,0:T(8,128)(2,1)}, f32[4,512,128]{2,1,0:T(8,128)}) custom-call(bf16[1024,512]{1,0:T(8,128)(2,1)} %q_ref.1, bf16[1024,512]{1,0:T(8,128)(2,1)} %v_ref.1, s32[4,1,1024]{2,1,0:T(1,128)} %reshape.9.codes_ref, bf16[4,512,128]{2,1,0:T(8,128)(2,1)} %cb_ref.1, bf16[512,2048]{1,0:T(8,128)(2,1)} %w_ref.1, ...), custom_call_target="tpu_custom_call" | custom-call | tf_op jit(solution)/shard_map/pallas_call | solution.py:325
  95.3 0.0 copy-start.1
  95.3 0.0 copy-start
  95.3 2.4 %copy.12 = bf16[1024,512]{1,0:T(8,128)(2,1)} copy(bf16[1024,512]{1,0:T(8,128)(2,1)} %get-tuple-element.6) | data formatting | bytes 2097152
  97.7 0.0 copy-done.1
  97.7 1.0 copy.13
  98.7 0.0 copy-done
  98.7 1.0 copy.14
Async XLA Ops:
  95.3 2.4 %copy-start.1 = (bf16[1024,512]{1,0:T(8,128)(2,1)S(1)}, bf16[1024,512]{1,0:T(8,128)(2,1)}, u32[]{:S(2)}) copy-start(bf16[1024,512]{1,0:T(8,128)(2,1)} %get-tuple-element.7) | copy-start | bytes 3145732
  95.3 3.4 %copy-start = (f32[4,512,128]{2,1,0:T(8,128)S(1)}, f32[4,512,128]{2,1,0:T(8,128)}, u32[]{:S(2)}) copy-start(f32[4,512,128]{2,1,0:T(8,128)} %get-tuple-element.8) | copy-start | bytes 3145732

commit v2 on v1

--- a/solution.py
+++ b/solution.py
@@ -1,4 +1,5 @@
 import functools
+import math
 
 import jax
 import jax.numpy as jnp
@@ -8,7 +9,7 @@
 from jax.sharding import PartitionSpec as P
 
 BLOCK = 512
-CHUNKS = 4
+HALF = BLOCK // 2
 NEG = -1e30
 F32 = jnp.float32
 BF16 = jnp.bfloat16
@@ -28,8 +29,9 @@
     q_ref, v_ref, codes_ref, cb_ref, w_ref, go_ref,
     gq_ref, gv_ref, gc_ref,
     gath, dout, hot_t, hot, keys, keys_t, own, cnt_block, cnt_send, cnt_recv, cnt_before,
-    p1_send, p1_recv, p2_send, p2_recv, local_part, vpart, s1_send, s1_recv, s2_send, s2_recv,
-    ag_s, ag_r, cn_s, cn_r, p1_s, p1_r, p2_s, p2_r, s1_s, s1_r, s2_s, s2_r,
+    counts_at, low, cache_low, local_part, vpart,
+    p1_send, p1_recv, p2_send, p2_recv, l1_send, l1_recv, l2_send, l2_recv, s1_send, s1_recv, s2_send, s2_recv,
+    ag_s, ag_r, cn_s, cn_r, p1_s, p1_r, p2_s, p2_r, l1_s, l1_r, l2_s, l2_r, s1_s, s1_r, s2_s, s2_r,
 ):
     rows_all = q_ref.shape[0]
     heads, entries, width = cb_ref.shape
@@ -61,7 +63,8 @@
         pl.semaphore_signal(barrier, inc=1, device_id={"head": flip(mine, b)}, device_id_type=MESH)
     pl.semaphore_wait(barrier, n_seq - 1 + len(bits))
 
-    piece = rows_all // CHUNKS
+    chunks = heads
+    piece = rows_all // chunks
 
     def gather_copy(src_mask, to, chunk):
         block = flip(mine, src_mask)
@@ -80,21 +83,18 @@
         known += [m ^ b for m in known]
     for m, b in plan:
         if m == 0:
-            for chunk in range(CHUNKS):
+            for chunk in range(chunks):
                 gather_copy(m, b, chunk).start()
-    by_slot = {m ^ b: (m, b) for m, b in plan}
-    taken = set()
-
-    def arrive(slot, chunk):
-        if (slot, chunk) not in taken:
-            taken.add((slot, chunk))
-            m, b = by_slot[slot]
-            gather_copy(m, b, chunk).wait_recv()
+    relayed = {m for m, b in plan if m != 0}
 
     def forward(chunk):
+        done = set()
         for m, b in plan:
             if m != 0:
-                arrive(m, chunk)
+                if m not in done:
+                    done.add(m)
+                    first, to = next((x, y) for x, y in plan if x ^ y == m)
+                    gather_copy(first, to, chunk).wait_recv()
                 gather_copy(m, b, chunk).start()
 
     gath[mine] = go_ref[...]
@@ -159,24 +159,71 @@
 
     over_peers(send_sums)
     p1_recv[me] = p1_send[me]
-    for chunk in range(CHUNKS // 2):
-        forward(chunk)
-    over_peers(lambda peer: prefix_out(peer, peer).wait_recv())
+    over_peers(lambda peer: count_copy(peer, peer).wait_recv())
+    cnt_before[...] = lax.fori_loop(0, me, lambda j, total: total + cnt_recv[j], jnp.zeros(cnt_before.shape, F32))
 
     def scan_step(j, total):
         p2_send[j] = total.astype(BF16)
         return total + p1_recv[j].astype(F32)
 
-    lax.fori_loop(0, n_seq, scan_step, jnp.zeros((heads, part, width), F32))
-    over_peers(lambda peer: prefix_back(peer, me).start())
-    p2_recv[me] = p2_send[me]
-    over_peers(lambda peer: count_copy(peer, peer).wait_recv())
-    cnt_before[...] = lax.fori_loop(0, me, lambda j, total: total + cnt_recv[j], jnp.zeros(cnt_before.shape, F32))
-    for chunk in range(CHUNKS // 2, CHUNKS):
-        forward(chunk)
-    for chunk in range(CHUNKS):
-        for slot in by_slot:
-            arrive(slot, chunk)
+    def scan_prefix():
+        over_peers(lambda peer: prefix_out(peer, peer).wait_recv())
+        lax.fori_loop(0, n_seq, scan_step, jnp.zeros((heads, part, width), F32))
+        over_peers(lambda peer: prefix_back(peer, me).start())
+        p2_recv[me] = p2_send[me]
+
+    tri = (lax.broadcasted_iota(jnp.int32, (HALF, HALF), 0) <= lax.broadcasted_iota(jnp.int32, (HALF, HALF), 1))
+    rate = scale * math.log2(math.e)
+
+    def wide(column):
+        return jnp.concatenate([column] * (HALF // width), axis=1)
+
+    def probabilities(h, carry):
+        head_lanes = pl.ds(pl.multiple_of(h * width, width), width)
+        book = cb_ref[h]
+        count_row = cnt_before[h]
+        for b in range(nb):
+            count_full = jnp.transpose(jnp.broadcast_to(count_row, (width, entries)))
+            counts_at[h, b] = count_full
+            counts = wide(count_full)
+            bias = wide(jnp.where(count_full > 0.0, 0.0, NEG))
+            for half in range(2):
+                upto = (half + 1) * HALF
+                cols = pl.ds(half * HALF, HALF)
+                query = q_ref[pl.ds(b * BLOCK + half * HALF, HALF), head_lanes]
+                diagonal = jnp.where(tri, nt(keys[h, b, half * HALF:upto], query), NEG)
+                cache_scores = nt(book, query) + bias
+                highest = jnp.maximum(
+                    jnp.max(diagonal, axis=0, keepdims=True), jnp.max(cache_scores, axis=0, keepdims=True))
+                if half:
+                    above = nt(keys[h, b, 0:HALF], query)
+                    highest = jnp.maximum(highest, jnp.max(above, axis=0, keepdims=True))
+                    above_exp = jnp.exp2((above - highest) * rate)
+                diagonal_exp = jnp.exp2((diagonal - highest) * rate)
+                cache_exp = jnp.exp2((cache_scores - highest) * rate)
+                total = (jnp.sum(diagonal_exp, axis=0, keepdims=True)
+                         + jnp.sum(cache_exp * counts, axis=0, keepdims=True))
+                if half:
+                    total = total + jnp.sum(above_exp, axis=0, keepdims=True)
+                inverse = 1.0 / total
+                low[h, b, half * HALF:upto, cols] = (diagonal_exp * inverse).astype(BF16)
+                if half:
+                    low[h, b, 0:HALF, cols] = (above_exp * inverse).astype(BF16)
+                cache_low[h, b, :, cols] = (cache_exp * inverse).astype(BF16)
+            count_row = count_row + cnt_block[h, b]
+        forward(h)
+
+        @pl.when(h == max(heads - 2, 0))
+        def _():
+            scan_prefix()
+
+        return carry
+
+    lax.fori_loop(0, heads, probabilities, 0)
+    for chunk in range(chunks):
+        for m, b in plan:
+            if m ^ b not in relayed:
+                gather_copy(m, b, chunk).wait_recv()
 
     depth = go_ref.shape[1]
 
@@ -189,6 +236,43 @@
         return carry
 
     lax.fori_loop(0, nb, project, 0)
+
+    def cache_parts(h, carry):
+        head_lanes = pl.ds(pl.multiple_of(h * width, width), width)
+        part_total = jnp.zeros((entries, width), F32)
+        for b in range(nb):
+            value_part = nn(cache_low[h, b], dout[pl.ds(b * BLOCK, BLOCK), head_lanes])
+            vpart[h, b] = value_part
+            part_total += value_part
+        l1_send[:, h] = part_total.astype(BF16).reshape(n_seq, part, width)
+        return carry
+
+    lax.fori_loop(0, heads, cache_parts, 0)
+
+    def suffix_out(to, source):
+        return pltpu.make_async_remote_copy(
+            src_ref=l1_send.at[to], dst_ref=l1_recv.at[source], send_sem=l1_s.at[to], recv_sem=l1_r.at[source],
+            device_id={"seq": to}, device_id_type=MESH)
+
+    def suffix_back(to, source):
+        return pltpu.make_async_remote_copy(
+            src_ref=l2_send.at[to], dst_ref=l2_recv.at[source], send_sem=l2_s.at[to], recv_sem=l2_r.at[source],
+            device_id={"seq": to}, device_id_type=MESH)
+
+    over_peers(lambda peer: suffix_out(peer, me).start())
+    l1_recv[me] = l1_send[me]
+
+    def later_step(k, total):
+        j = n_seq - 1 - k
+        l2_send[j] = total.astype(BF16)
+        return total + l1_recv[j].astype(F32)
+
+    def scan_suffix():
+        over_peers(lambda peer: suffix_out(peer, peer).wait_recv())
+        lax.fori_loop(0, n_seq, later_step, jnp.zeros((heads, part, width), F32))
+        over_peers(lambda peer: suffix_back(peer, me).start())
+        l2_recv[me] = l2_send[me]
+
     over_peers(lambda peer: prefix_back(peer, peer).wait_recv())
 
     def late_out(h, to, source):
@@ -199,7 +283,7 @@
 
     def late_back(h, to, source):
         return pltpu.make_async_remote_copy(
-            src_ref=s2_send.at[h, to], dst_ref=s2_recv.at[h, source],
+            src_ref=s2_send.at[h], dst_ref=s2_recv.at[h, source],
             send_sem=s2_s.at[h, to], recv_sem=s2_r.at[h, source],
             device_id={"seq": to}, device_id_type=MESH)
 
@@ -207,73 +291,58 @@
         over_peers(lambda peer: late_out(h, peer, peer).wait_recv())
 
         def code_step(j, total):
-            return total + s1_recv[h, j, 1].astype(F32)
-
-        code = lax.fori_loop(0, n_seq, code_step, jnp.zeros((part, width), F32)).astype(BF16)
-
-        def later_step(k, total):
-            j = n_seq - 1 - k
-            s2_send[h, j, 0] = total.astype(BF16)
-            s2_send[h, j, 1] = code
-            return total + s1_recv[h, j, 0].astype(F32)
-
-        lax.fori_loop(0, n_seq, later_step, jnp.zeros((part, width), F32))
+            return total + s1_recv[h, j].astype(F32)
+
+        s2_send[h] = lax.fori_loop(0, n_seq, code_step, jnp.zeros((part, width), F32)).astype(BF16)
         over_peers(lambda peer: late_back(h, peer, me).start())
-        s2_recv[h, me] = s2_send[h, me]
+        s2_recv[h, me] = s2_send[h]
 
     def attend(h, carry):
         head_lanes = pl.ds(pl.multiple_of(h * width, width), width)
         book = cb_ref[h]
         book_t = jnp.transpose(book.astype(F32)).astype(BF16)
         prefix = p2_recv[:, h].astype(F32).reshape(entries, width)
-        count_row = cnt_before[h]
-        code_total = jnp.zeros((entries, width), F32)
-        part_total = jnp.zeros((entries, width), F32)
+        from_cache = jnp.zeros((entries, width), F32)
+        from_keys = jnp.zeros((entries, width), F32)
         for b in range(nb):
-            rows = pl.ds(b * BLOCK, BLOCK)
-            query = q_ref[rows, head_lanes]
-            value = v_ref[rows, head_lanes]
-            grad = dout[rows, head_lanes]
-            key = keys[h, b]
             cache_values = prefix.astype(BF16)
-            count_full = jnp.transpose(jnp.broadcast_to(count_row, (width, entries)))
-            bias_full = jnp.where(count_full > 0.0, 0.0, NEG)
-            counts = jnp.concatenate([count_full] * (BLOCK // width), axis=1)
-            bias = jnp.concatenate([bias_full] * (BLOCK // width), axis=1)
-            at_u = lax.broadcasted_iota(jnp.int32, (BLOCK, BLOCK), 0)
-            at_t = lax.broadcasted_iota(jnp.int32, (BLOCK, BLOCK), 1)
-            scores = jnp.where(at_u <= at_t, nt(key, query) * scale, NEG)
-            cache_scores = nt(book, query) * scale + bias
-            highest = jnp.maximum(
-                jnp.max(scores, axis=0, keepdims=True), jnp.max(cache_scores, axis=0, keepdims=True))
-            local_exp = jnp.exp(scores - highest)
-            cache_exp = jnp.exp(cache_scores - highest)
-            total = jnp.sum(local_exp, axis=0, keepdims=True) + jnp.sum(cache_exp * counts, axis=0, keepdims=True)
-            inverse = 1.0 / total
-            local_prob = local_exp * inverse
-            cache_prob = cache_exp * inverse
-            local_low = local_prob.astype(BF16)
-            cache_low = cache_prob.astype(BF16)
-            local_grad = nt(value, grad)
-            cache_grad = nt(cache_values, grad)
-            delta = (jnp.sum(local_low.astype(F32) * local_grad, axis=0, keepdims=True)
-                     + jnp.sum(cache_low.astype(F32) * cache_grad, axis=0, keepdims=True))
-            local_score_grad = (local_prob * (local_grad - delta) * scale).astype(BF16)
-            cache_score_grad = (cache_prob * (cache_grad - delta * counts) * scale).astype(BF16)
-            gq_t = nn(keys_t[h, b], local_score_grad) + nn(book_t, cache_score_grad)
-            gq_ref[rows, head_lanes] = jnp.transpose(gq_t).astype(BF16)
-            key_grad = nn(local_score_grad, query).astype(BF16)
-            code_total += nn(hot_t[h, b], key_grad) + nn(cache_score_grad, query)
-            value_part = nn(cache_low, grad)
-            vpart[h, b] = value_part
-            part_total += value_part
-            local_part[h, b] = nn(local_low, grad)
+            counts = wide(counts_at[h, b])
+            key_parts = []
+            value_parts = []
+            for half in range(2):
+                upto = (half + 1) * HALF
+                cols = pl.ds(half * HALF, HALF)
+                rows = pl.ds(b * BLOCK + half * HALF, HALF)
+                query = q_ref[rows, head_lanes]
+                grad = dout[rows, head_lanes]
+                local_grad = nt(v_ref[pl.ds(b * BLOCK, upto), head_lanes], grad)
+                cache_grad = nt(cache_values, grad)
+                local_low = low[h, b, 0:upto, cols]
+                local_prob = local_low.astype(F32)
+                cache_prob = cache_low[h, b, :, cols].astype(F32)
+                delta = (jnp.sum(local_prob * local_grad, axis=0, keepdims=True)
+                         + jnp.sum(cache_prob * cache_grad, axis=0, keepdims=True))
+                local_score_grad = (local_prob * (local_grad - delta)).astype(BF16)
+                cache_score_grad = (cache_prob * (cache_grad - delta * counts)).astype(BF16)
+                gq_t = nn(keys_t[h, b, :, 0:upto], local_score_grad) + nn(book_t, cache_score_grad)
+                gq_ref[rows, head_lanes] = jnp.transpose(gq_t * scale).astype(BF16)
+                key_parts.append(nn(local_score_grad, query))
+                value_parts.append(nn(local_low, grad))
+                from_cache += nn(cache_score_grad, query)
+            for at, parts in enumerate((key_parts, value_parts)):
+                joined = jnp.concatenate([parts[0] + parts[1][:HALF], parts[1][HALF:]], axis=0)
+                if at:
+                    local_part[h, b] = joined
+                else:
+                    from_keys += nn(hot_t[h, b], (joined * scale).astype(BF16))
             prefix = prefix + own[h, b]
-            count_row = count_row + cnt_block[h, b]
-        s1_send[h, :, 0] = part_total.astype(BF16).reshape(n_seq, part, width)
-        s1_send[h, :, 1] = code_total.astype(BF16).reshape(n_seq, part, width)
+        s1_send[h] = (from_keys + from_cache * scale).astype(BF16).reshape(n_seq, part, width)
         s1_recv[h, me] = s1_send[h, me]
         over_peers(lambda peer: late_out(h, peer, me).start())
+
+        @pl.when(h == min(1, heads - 1))
+        def _():
+            scan_suffix()
 
         @pl.when(h >= 1)
         def _():
@@ -282,32 +351,46 @@
         return carry
 
     lax.fori_loop(0, heads, attend, 0)
-    combine(heads - 1)
+    over_peers(lambda peer: suffix_back(peer, peer).wait_recv())
 
     def finish(h, carry):
         head_lanes = pl.ds(pl.multiple_of(h * width, width), width)
-        over_peers(lambda peer: late_back(h, peer, peer).wait_recv())
-        gc_ref[h] = s2_recv[h, :, 1].astype(F32).reshape(entries, width)
-        later = s2_recv[h, :, 0].astype(F32).reshape(entries, width)
+        later = l2_recv[:, h].astype(F32).reshape(entries, width)
         for b in reversed(range(nb)):
             rows = pl.ds(b * BLOCK, BLOCK)
             lookup = nn(hot[h, b], later.astype(BF16))
             gv_ref[rows, head_lanes] = (local_part[h, b] + lookup).astype(BF16)
             later = later + vpart[h, b]
+
+        @pl.when(h == heads - 2)
+        def _():
+            combine(heads - 1)
+
+        return carry
+
+    lax.fori_loop(0, heads, finish, 0)
+    if heads == 1:
+        combine(0)
+
+    def release(h, carry):
+        over_peers(lambda peer: late_back(h, peer, peer).wait_recv())
+        gc_ref[h] = s2_recv[h].astype(F32).reshape(entries, width)
         over_peers(lambda peer: late_out(h, peer, me).wait_send())
         over_peers(lambda peer: late_back(h, peer, me).wait_send())
         return carry
 
-    lax.fori_loop(0, heads, finish, 0)
+    lax.fori_loop(0, heads, release, 0)
 
     def drain(peer):
         prefix_out(peer, me).wait_send()
         prefix_back(peer, me).wait_send()
         count_copy(peer, me).wait_send()
+        suffix_out(peer, me).wait_send()
+        suffix_back(peer, me).wait_send()
 
     over_peers(drain)
     for m, b in plan:
-        for chunk in range(CHUNKS):
+        for chunk in range(chunks):
             gather_copy(m, b, chunk).wait_send()
 
 
@@ -320,7 +403,7 @@
     codes_t = codes.T.reshape(heads, 1, row_count)
     vmem = pl.BlockSpec(memory_space=pltpu.VMEM)
     dma = pltpu.SemaphoreType.DMA
-    late = pltpu.VMEM((heads, n_seq, 2, part, width), BF16)
+    late = pltpu.VMEM((heads, n_seq, part, width), BF16)
     early = pltpu.VMEM((n_seq, heads, part, width), BF16)
     return pl.pallas_call(
         functools.partial(kernel, n_seq, n_head),
@@ -343,11 +426,17 @@
             pltpu.VMEM((heads, 1, entries), F32),
             pltpu.VMEM((n_seq, heads, 1, entries), F32),
             pltpu.VMEM((heads, 1, entries), F32),
-            early, early, early, early,
+            pltpu.VMEM((heads, nb, entries, width), F32),
+            pltpu.VMEM((heads, nb, BLOCK, BLOCK), BF16),
+            pltpu.VMEM((heads, nb, entries, BLOCK), BF16),
             pltpu.VMEM((heads, nb, BLOCK, width), F32),
             pltpu.VMEM((heads, nb, entries, width), F32),
-            late, late, late, late,
-            dma((n_head, CHUNKS)), dma((n_head, CHUNKS)),
+            early, early, early, early,
+            early, early, early, early,
+            late, late, pltpu.VMEM((heads, part, width), BF16), late,
+            dma((n_head, heads)), dma((n_head, heads)),
+            dma((n_seq,)), dma((n_seq,)),
+            dma((n_seq,)), dma((n_seq,)),
             dma((n_seq,)), dma((n_seq,)),
             dma((n_seq,)), dma((n_seq,)),
             dma((n_seq,)), dma((n_seq,)),

time: 99.9 us -> 103 us (1.031)
  Pallas kernels: 93.3 us -> 96.8 us
    pallas_call x1, Pallas kernels: 93.3 us -> 96.8 us  [per_device(): pl.pallas_call(functools.partial(kernel, n_seq, n_head), out_shape=(jax.S...]
where the time goes in v2:
time: 103 us
  Pallas kernels  96.8 us (94%)
  local copies, waits for them, and re-layouts  5.69 us (6%)
    pallas_call x1, Pallas kernels, per_device(): pl.pallas_call(functools.partial(kernel, n_seq, n_head), out_shape=(jax.S...  96.8 us
    unnamed x7, local copies, waits for them, and re-layouts  4.36 us

profile of v2, /device:TPU:0, one launch (start us, length us, event | category | flops | bytes accessed | tf_op | source)
XLA Modules:
  0.0 103.1 jit_solution(7251154608551372805)
XLA Ops:
  0.6 1.3 %reshape.9.codes_ref = s32[4,1,1024]{2,1,0:T(1,128)} reshape(s32[4,1024]{1,0:T(4,128)} %bitcast.1) | data formatting | bytes 32768 | tf_op jit(solution)/shard_map/reshape | solution.py:403
  2.0 96.8 %shard_map.85 = (bf16[1024,512]{1,0:T(8,128)(2,1)}, bf16[1024,512]{1,0:T(8,128)(2,1)}, f32[4,512,128]{2,1,0:T(8,128)}) custom-call(bf16[1024,512]{1,0:T(8,128)(2,1)} %q_ref.1, bf16[1024,512]{1,0:T(8,128)(2,1)} %v_ref.1, s32[4,1,1024]{2,1,0:T(1,128)} %reshape.9.codes_ref, bf16[4,512,128]{2,1,0:T(8,128)(2,1)} %cb_ref.1, bf16[512,2048]{1,0:T(8,128)(2,1)} %w_ref.1, ...), custom_call_target="tpu_custom_call" | custom-call | tf_op jit(solution)/shard_map/pallas_call | solution.py:408
  98.7 0.0 copy-start.1
  98.7 0.0 copy-start
  98.7 2.4 %copy.12 = bf16[1024,512]{1,0:T(8,128)(2,1)} copy(bf16[1024,512]{1,0:T(8,128)(2,1)} %get-tuple-element.6) | data formatting | bytes 2097152
  101.2 0.0 copy-done.1
  101.2 1.0 copy.13
  102.1 0.0 copy-done
  102.1 1.0 copy.14
Async XLA Ops:
  98.7 2.4 %copy-start.1 = (bf16[1024,512]{1,0:T(8,128)(2,1)S(1)}, bf16[1024,512]{1,0:T(8,128)(2,1)}, u32[]{:S(2)}) copy-start(bf16[1024,512]{1,0:T(8,128)(2,1)} %get-tuple-element.7) | copy-start | bytes 3145732
  98.7 3.4 %copy-start = (f32[4,512,128]{2,1,0:T(8,128)S(1)}, f32[4,512,128]{2,1,0:T(8,128)}, u32[]{:S(2)}) copy-start(f32[4,512,128]{2,1,0:T(8,128)} %get-tuple-element.8) | copy-start | bytes 3145732
